TPU v7x, 32 devices: a whole 2x2x4 slice. The times are simulated.
32 devices in a mesh: batch: 2 (over x), ctx: 4 (over y, core), mp: 4 (over z).
Axes of the slice: x: 2, y: 2, z: 4, core: 2. Of those that a mesh axis runs over, the one named last changes fastest.
Arguments:
- hidden_in: bfloat16 [4, 512, 1024], P('batch', 'ctx'), may hold values from -6 to 6
- segment_ids: int32 [4, 512], P('batch', 'ctx'), may hold values from 0 to 3, never falling along the last dimension, each value on 1 to 256 neighbouring positions
- gains: bfloat16 [2, 2, 1024], P(None, None, ('batch', 'ctx', 'mp')), may hold values from 0.5 to 1.5
- biases: bfloat16 [2, 10, 1024], P(None, None, ('batch', 'ctx', 'mp')), may hold values from -3 to 3
- w_qkv: bfloat16 [2, 1024, 3, 1024], P(None, ('batch', 'ctx'), None, 'mp'), may hold values from -0.1875 to 0.1875
- w_out_t: bfloat16 [2, 1024, 1024], P(None, ('batch', 'ctx'), 'mp'), may hold values from -0.5 to 0.5
- w_up: bfloat16 [2, 1024, 4096], P(None, ('batch', 'ctx'), 'mp'), may hold values from -0.1875 to 0.1875
- w_down_t: bfloat16 [2, 1024, 4096], P(None, ('batch', 'ctx'), 'mp'), may hold values from -0.09375 to 0.09375
- grad_out: bfloat16 [4, 512, 1024], P('batch', 'ctx'), may hold values from -6 to 6
Outputs:
- output: bfloat16 [4, 512, 1024], P('batch', 'ctx')
- grad_in: bfloat16 [4, 512, 1024], P('batch', 'ctx')
- grad_gains: float32 [2, 2, 1024], P(None, None, ('batch', 'ctx', 'mp'))
- grad_biases: float32 [2, 10, 1024], P(None, None, ('batch', 'ctx', 'mp'))
- grad_qkv: float32 [2, 1024, 3, 1024], P(None, ('batch', 'ctx'), None, 'mp')
- grad_attn_out: float32 [2, 1024, 1024], P(None, ('batch', 'ctx'), 'mp')
- grad_up: float32 [2, 1024, 4096], P(None, ('batch', 'ctx'), 'mp')
- grad_down: float32 [2, 1024, 4096], P(None, ('batch', 'ctx'), 'mp')
Inputs may be any that keep to these rules, and one draw needn't show every extreme that they name: `segment_ids`: document numbers never fall along a sequence; every document spans 1 to 256 tokens, and one of each sequence spans exactly that many.
All inputs are finite; a program needn't handle non-finite values.
Results may differ from a plain program's by a relative error of at most 0.023.
Values may be sent and summed in bfloat16 or wider, within the bound.
A program may use at most 128 MiB of HBM per device.

v0:
```python
import math
import jax
import jax.numpy as jnp
from jax import lax
from jax.sharding import PartitionSpec as P

HEADS = 16
HEAD = 64
EPS = 1e-05
GELU_C = 0.7978845608028654
GELU_K = 0.044715


def norm_parts(values):
    center = values - jnp.mean(values, -1, keepdims=True)
    inverse = lax.rsqrt(jnp.mean(center * center, -1, keepdims=True) + EPS)
    return (center * inverse, inverse)


def norm_back(grad_y, normed, inverse, gain):
    scaled = grad_y * gain
    return inverse * (
        scaled
        - jnp.mean(scaled, -1, keepdims=True)
        - normed * jnp.mean(scaled * normed, -1, keepdims=True)
    )


def gelu_parts(values):
    bend = jnp.tanh(GELU_C * (values + GELU_K * values * values * values))
    return (0.5 * values * (1.0 + bend), bend)


def gelu_slope(values, bend):
    return 0.5 * (1.0 + bend) + 0.5 * values * (1.0 - bend * bend) * GELU_C * (
        1.0 + 3.0 * GELU_K * values * values
    )


def block_mask(q_pos, q_seg, key_seg, start, block):
    k_pos = start + jnp.arange(block, dtype=jnp.int32)
    seg_keys = lax.dynamic_slice_in_dim(key_seg, start, block, 1)
    mask = (k_pos[None, None, :] <= q_pos[None, :, None]) & (
        seg_keys[:, None, :] == q_seg[:, :, None]
    )
    return mask[:, None]


def block_scores(query, keys, q_pos, start, block, slope, scale):
    k_pos = start + jnp.arange(block, dtype=jnp.int32)
    dist = (q_pos[:, None] - k_pos[None, :]).astype(jnp.float32)
    score = jnp.einsum("sqhd,skhd->shqk", query, keys, preferred_element_type=jnp.float32)
    return score * scale - slope[None, :, None, None] * dist[None, None]


def attend_forward(query, kv_all, q_pos, q_seg, key_seg, slope):
    seqs, rows, heads, width = query.shape
    length = kv_all.shape[1]
    block = min(512, length)
    scale = 1.0 / math.sqrt(width)

    def step(carry, index):
        start = index * block
        mask = block_mask(q_pos, q_seg, key_seg, start, block)

        def work(state):
            acc, total = state
            pair = lax.dynamic_slice_in_dim(kv_all, start, block, 1).reshape(
                seqs, block, 2, heads, width
            )
            score = block_scores(query, pair[:, :, 0], q_pos, start, block, slope, scale)
            expo = jnp.where(mask, jnp.exp(jnp.where(mask, score, 0.0)), 0.0)
            acc = acc + jnp.einsum(
                "shqk,skhd->sqhd",
                expo.astype(jnp.bfloat16),
                pair[:, :, 1],
                preferred_element_type=jnp.float32,
            )
            return (acc, total + jnp.sum(expo, -1))

        return (lax.cond(jnp.any(mask), work, lambda state: state, carry), None)

    init = (jnp.zeros(query.shape, jnp.float32), jnp.zeros((seqs, heads, rows), jnp.float32))
    (acc, total), _ = lax.scan(step, init, jnp.arange(length // block, dtype=jnp.int32))
    ctx = (acc / jnp.transpose(total, (0, 2, 1))[..., None]).astype(jnp.bfloat16)
    return (ctx, jnp.log(total))


def attend_backward(query, kv_all, q_pos, q_seg, key_seg, slope, ctx, lse, dctx):
    seqs, rows, heads, width = query.shape
    length = kv_all.shape[1]
    block = min(512, length)
    scale = 1.0 / math.sqrt(width)
    delta = jnp.transpose(
        jnp.sum(dctx.astype(jnp.float32) * ctx.astype(jnp.float32), -1), (0, 2, 1)
    )

    def step(carry, index):
        start = index * block
        mask = block_mask(q_pos, q_seg, key_seg, start, block)

        def work(state):
            grad_q, grad_kv = state
            pair = lax.dynamic_slice_in_dim(kv_all, start, block, 1).reshape(
                seqs, block, 2, heads, width
            )
            score = block_scores(query, pair[:, :, 0], q_pos, start, block, slope, scale)
            prob = jnp.where(mask, jnp.exp(jnp.where(mask, score - lse[..., None], 0.0)), 0.0)
            grad_v = jnp.einsum(
                "shqk,sqhd->skhd",
                prob.astype(jnp.bfloat16),
                dctx,
                preferred_element_type=jnp.float32,
            )
            grad_p = jnp.einsum(
                "sqhd,skhd->shqk", dctx, pair[:, :, 1], preferred_element_type=jnp.float32
            )
            grad_s = (prob * (grad_p - delta[..., None])).astype(jnp.bfloat16)
            grad_q = (
                grad_q
                + jnp.einsum(
                    "shqk,skhd->sqhd", grad_s, pair[:, :, 0], preferred_element_type=jnp.float32
                )
                * scale
            )
            grad_k = (
                jnp.einsum("shqk,sqhd->skhd", grad_s, query, preferred_element_type=jnp.float32)
                * scale
            )
            piece = jnp.stack([grad_k, grad_v], 2).reshape(seqs, block, 2, heads * width)
            return (grad_q, lax.dynamic_update_slice_in_dim(grad_kv, piece, start, 1))

        return (lax.cond(jnp.any(mask), work, lambda state: state, carry), None)

    init = (
        jnp.zeros(query.shape, jnp.float32),
        jnp.zeros((seqs, length, 2, heads * width), jnp.float32),
    )
    (grad_q, grad_kv), _ = lax.scan(step, init, jnp.arange(length // block, dtype=jnp.int32))
    return (grad_q, grad_kv)


def per_device(hidden_in, segment_ids, gains, biases, w_qkv, w_out_t, w_up, w_down_t, grad_out):
    seqs, rows, width = hidden_in.shape
    layers = w_qkv.shape[0]
    cols = w_qkv.shape[3]
    ff_cols = w_up.shape[2]
    heads = cols // HEAD
    mp_count = lax.axis_size("mp")
    mp_index = lax.axis_index("mp")
    all_gains, all_biases = (
        lax.all_gather(gains, ("batch", "ctx", "mp"), axis=2, tiled=True),
        lax.all_gather(biases, ("batch", "ctx", "mp"), axis=2, tiled=True),
    )
    key_seg = lax.all_gather(segment_ids, "ctx", axis=1, tiled=True)
    q_pos = lax.axis_index("ctx") * rows + jnp.arange(rows, dtype=jnp.int32)
    head_ids = (mp_index * heads + jnp.arange(heads, dtype=jnp.int32)).astype(jnp.float32)
    slope = jnp.exp2(-8.0 * (head_ids + 1.0) / HEADS)
    own = (jnp.arange(width, dtype=jnp.int32) // cols == mp_index).astype(jnp.float32)
    full_ff = ff_cols * mp_count

    def place(values, offset, total):
        return lax.dynamic_update_slice_in_dim(jnp.zeros((total,), jnp.float32), values, offset, 0)

    def unpack(layer):
        vec = all_biases[layer]
        query_bias = lax.dynamic_slice_in_dim(vec[2], mp_index * cols, cols, 0)
        value_bias = lax.dynamic_slice_in_dim(vec[3], mp_index * cols, cols, 0)
        up_projection_bias = lax.dynamic_slice_in_dim(
            vec[6:].reshape(-1), mp_index * ff_cols, ff_cols, 0
        )
        return (vec, query_bias, value_bias, up_projection_bias)

    def forward_layer(layer, state, weights):
        query_weight, w_o, up_weight, w_d = weights
        vec, query_bias, value_bias, up_projection_bias = unpack(layer)
        normed1, _ = norm_parts(state)
        first_activation = (normed1 * all_gains[layer, 0] + vec[0]).astype(jnp.bfloat16)
        query_key_value = jnp.einsum(
            "bph,hue->bpue", first_activation, query_weight, preferred_element_type=jnp.float32
        )
        shift = jnp.stack([query_bias, jnp.zeros_like(query_bias), value_bias])
        qkv_bf = (query_key_value + shift).astype(jnp.bfloat16)
        kv_all = lax.all_gather(qkv_bf[:, :, 1:], "ctx", axis=1, tiled=True)
        query = qkv_bf[:, :, 0].reshape(seqs, rows, heads, HEAD)
        ctx, lse = attend_forward(query, kv_all, q_pos, segment_ids, key_seg, slope)
        ctx_flat = ctx.reshape(seqs, rows, cols)
        part = jnp.einsum("slc,oc->slo", ctx_flat, w_o, preferred_element_type=jnp.float32)
        mid = state + lax.psum(part, "mp") + vec[4]
        normed2, _ = norm_parts(mid)
        second_activation = (normed2 * all_gains[layer, 1] + vec[1]).astype(jnp.bfloat16)
        up_projected = (
            jnp.einsum(
                "nhz,zb->nhb", second_activation, up_weight, preferred_element_type=jnp.float32
            )
            + up_projection_bias
        )
        act, _ = gelu_parts(up_projected)
        act_bf = act.astype(jnp.bfloat16)
        down = jnp.einsum("slf,of->slo", act_bf, w_d, preferred_element_type=jnp.float32)
        result = mid + lax.psum(down, "mp") + vec[5]
        return (
            result,
            (
                state,
                first_activation,
                qkv_bf,
                kv_all,
                ctx_flat,
                lse,
                mid,
                second_activation,
                up_projected,
                act_bf,
            ),
        )

    state = hidden_in.astype(jnp.float32)
    saves = []
    for layer in range(layers):
        weights = (
            lax.all_gather(w_qkv[layer], ("batch", "ctx"), axis=0, tiled=True),
            lax.all_gather(w_out_t[layer], ("batch", "ctx"), axis=0, tiled=True),
            lax.all_gather(w_up[layer], ("batch", "ctx"), axis=0, tiled=True),
            lax.all_gather(w_down_t[layer], ("batch", "ctx"), axis=0, tiled=True),
        )
        state, saved = forward_layer(layer, state, weights)
        saves.append((weights, saved))
    output = state.astype(jnp.bfloat16)
    grad = grad_out.astype(jnp.float32)
    gain_rows = [None] * layers
    bias_rows = [None] * layers
    matrix_grads = [None] * layers
    for layer in reversed(range(layers)):
        kept_weights, saved = saves[layer]
        (
            x_in,
            first_activation,
            qkv_bf,
            kv_kept,
            ctx_flat,
            lse,
            mid,
            second_activation,
            up_projected,
            act_bf,
        ) = saved
        query_weight, w_o, up_weight, w_d = (
            lax.all_gather(w_qkv[layer], ("batch", "ctx"), axis=0, tiled=True),
            lax.all_gather(w_out_t[layer], ("batch", "ctx"), axis=0, tiled=True),
            lax.all_gather(w_up[layer], ("batch", "ctx"), axis=0, tiled=True),
            lax.all_gather(w_down_t[layer], ("batch", "ctx"), axis=0, tiled=True),
        )
        kv_all = lax.all_gather(qkv_bf[:, :, 1:], "ctx", axis=1, tiled=True)
        gain1 = all_gains[layer, 0]
        gain2 = all_gains[layer, 1]
        grad_bf = grad.astype(jnp.bfloat16)
        grad_bd = jnp.sum(grad, (0, 1))
        grad_wd = jnp.einsum("slo,slf->of", grad_bf, act_bf, preferred_element_type=jnp.float32)
        dact = jnp.einsum("slo,of->slf", grad_bf, w_d, preferred_element_type=jnp.float32)
        _, bend = gelu_parts(up_projected)
        dup = dact * gelu_slope(up_projected, bend)
        grad_bu = jnp.sum(dup, (0, 1))
        up_gradient_half_precision = dup.astype(jnp.bfloat16)
        up_weight_gradient = jnp.einsum(
            "qwi,qwn->in",
            second_activation,
            up_gradient_half_precision,
            preferred_element_type=jnp.float32,
        )
        da2 = lax.psum(
            jnp.einsum(
                "cju,xu->cjx",
                up_gradient_half_precision,
                up_weight,
                preferred_element_type=jnp.float32,
            ),
            "mp",
        )
        normed2, inverse2 = norm_parts(mid)
        grad_g2 = jnp.sum(da2 * normed2, (0, 1))
        grad_b2 = jnp.sum(da2, (0, 1))
        gx2 = grad + norm_back(da2, normed2, inverse2, gain2)
        grad_bo = jnp.sum(gx2, (0, 1))
        gx2_bf = gx2.astype(jnp.bfloat16)
        grad_wo = jnp.einsum("slo,slc->oc", gx2_bf, ctx_flat, preferred_element_type=jnp.float32)
        dctx = jnp.einsum("slo,oc->slc", gx2_bf, w_o, preferred_element_type=jnp.float32).astype(
            jnp.bfloat16
        )
        query = qkv_bf[:, :, 0].reshape(seqs, rows, heads, HEAD)
        ctx_heads = ctx_flat.reshape(seqs, rows, heads, HEAD)
        dctx_heads = dctx.reshape(seqs, rows, heads, HEAD)
        grad_q, grad_kv_terms = attend_backward(
            query, kv_all, q_pos, segment_ids, key_seg, slope, ctx_heads, lse, dctx_heads
        )
        grad_kv = lax.psum_scatter(grad_kv_terms, "ctx", scatter_dimension=1, tiled=True)
        grad_qf = grad_q.reshape(seqs, rows, cols)
        grad_bq = jnp.sum(grad_qf, (0, 1))
        value_bias_gradient = jnp.sum(grad_kv[:, :, 1], (0, 1))
        packed_projection_gradient = jnp.concatenate([grad_qf[:, :, None], grad_kv], 2).astype(
            jnp.bfloat16
        )
        query_weight_gradient = jnp.einsum(
            "ebz,ebpy->zpy",
            first_activation,
            packed_projection_gradient,
            preferred_element_type=jnp.float32,
        )
        da1 = lax.psum(
            jnp.einsum(
                "aewu,vwu->aev",
                packed_projection_gradient,
                query_weight,
                preferred_element_type=jnp.float32,
            ),
            "mp",
        )
        normed1, inverse1 = norm_parts(x_in)
        grad_g1 = jnp.sum(da1 * normed1, (0, 1))
        grad_b1 = jnp.sum(da1, (0, 1))
        grad = gx2 + norm_back(da1, normed1, inverse1, gain1)
        gain_rows[layer] = jnp.stack([grad_g1 * own, grad_g2 * own])
        head_rows = jnp.stack(
            [
                grad_b1 * own,
                grad_b2 * own,
                place(grad_bq, mp_index * cols, width),
                place(value_bias_gradient, mp_index * cols, width),
                grad_bo * own,
                grad_bd * own,
            ]
        )
        unit_rows = place(grad_bu, mp_index * ff_cols, full_ff).reshape(full_ff // width, width)
        bias_rows[layer] = jnp.concatenate([head_rows, unit_rows], 0)
        matrix_grads[layer] = (
            lax.psum_scatter(
                query_weight_gradient.astype(jnp.bfloat16),
                ("batch", "ctx"),
                scatter_dimension=0,
                tiled=True,
            ).astype(jnp.float32),
            lax.psum_scatter(
                grad_wo.astype(jnp.bfloat16), ("batch", "ctx"), scatter_dimension=0, tiled=True
            ).astype(jnp.float32),
            lax.psum_scatter(
                up_weight_gradient.astype(jnp.bfloat16),
                ("batch", "ctx"),
                scatter_dimension=0,
                tiled=True,
            ).astype(jnp.float32),
            lax.psum_scatter(
                grad_wd.astype(jnp.bfloat16), ("batch", "ctx"), scatter_dimension=0, tiled=True
            ).astype(jnp.float32),
        )
    grad_gains, grad_biases = (
        lax.psum_scatter(
            jnp.stack(gain_rows), ("batch", "ctx", "mp"), scatter_dimension=2, tiled=True
        ),
        lax.psum_scatter(
            jnp.stack(bias_rows), ("batch", "ctx", "mp"), scatter_dimension=2, tiled=True
        ),
    )
    grad_qkv = jnp.stack([item[0] for item in matrix_grads])
    grad_attn_out = jnp.stack([item[1] for item in matrix_grads])
    grad_up = jnp.stack([item[2] for item in matrix_grads])
    grad_down = jnp.stack([item[3] for item in matrix_grads])
    return (
        output,
        grad.astype(jnp.bfloat16),
        grad_gains,
        grad_biases,
        grad_qkv,
        grad_attn_out,
        grad_up,
        grad_down,
    )


def solution(mesh):
    in_specs = (
        P("batch", "ctx", None),
        P("batch", "ctx"),
        P(None, None, ("batch", "ctx", "mp")),
        P(None, None, ("batch", "ctx", "mp")),
        P(None, ("batch", "ctx"), None, "mp"),
        P(None, ("batch", "ctx"), "mp"),
        P(None, ("batch", "ctx"), "mp"),
        P(None, ("batch", "ctx"), "mp"),
        P("batch", "ctx", None),
    )
    out_specs = (
        P("batch", "ctx", None),
        P("batch", "ctx", None),
        P(None, None, ("batch", "ctx", "mp")),
        P(None, None, ("batch", "ctx", "mp")),
        P(None, ("batch", "ctx"), None, "mp"),
        P(None, ("batch", "ctx"), "mp"),
        P(None, ("batch", "ctx"), "mp"),
        P(None, ("batch", "ctx"), "mp"),
    )
    return jax.shard_map(
        per_device, mesh=mesh, in_specs=in_specs, out_specs=out_specs, check_vma=False
    )
```

profile of v0, /device:TPU:0, one launch (start us, length us, event | category | flops | bytes accessed | tf_op | source)
XLA Modules:
  0.0 1558.1 jit_solution(14924374231961429402)
XLA Ops:
  10.7 74.2 %all_gather.51 = bf16[2,10,1024]{1,0,2:T(2,128)(2,1)S(1)} all-gather(bf16[2,10,32]{1,0,2:T(2,128)(2,1)S(1)} %copy.109), channel_id=1, replica_groups=mesh['batch'=2,'ctx'=4,'mp'=4] {'batch','ctx','mp'}, dimensions={2}, use_global_device_ids=true | all-gather | bytes 42240 | tf_op jit(solution)/shard_map/all_gather | solution.py:153
  84.8 2.5 fusion.155
  89.5 68.0 %all_gather.50 = bf16[2,2,1024]{1,0,2:T(2,128)(2,1)S(1)} all-gather(bf16[2,2,32]{1,0,2:T(2,128)(2,1)S(1)} %copy.108), channel_id=1, replica_groups=mesh['batch'=2,'ctx'=4,'mp'=4] {'batch','ctx','mp'}, dimensions={2}, use_global_device_ids=true | all-gather | bytes 8448 | tf_op jit(solution)/shard_map/all_gather | solution.py:152
  158.0 18.2 %fusion.103 = (f32[1024]{0:T(1024)S(1)}, f32[1024]{0:T(1024)S(1)}, f32[1024]{0:T(1024)S(1)}, f32[1024]{0:T(1024)S(1)}) fusion(bf16[2,2,1024]{1,0,2:T(2,128)(2,1)S(1)} %all_gather.50), kind=kLoop, calls=%fused_computation.161 | loop fusion | flops 4096 | bytes 24576 | tf_op jit(solution)/shard_map/mul | solution.py:191
  176.3 24.6 %fusion.101 = (f32[1024]{0:T(1024)}, f32[1024]{0:T(1024)}, f32[1024]{0:T(1024)}, f32[1024]{0:T(1024)S(1)}, f32[1024]{0:T(1024)S(1)}, /*index=5*/f32[1024]{0:T(1024)S(1)}, f32[1024]{0:T(1024)S(1)}, f32[1024]{0:T(1024)S(1)}) fusion(bf16[2,10,1024]{1,0,2:T(2,128)(2,1)S(1)} %all_gather.51), kind=kLoop, calls=%fused_computation.157 | loop fusion | flops 8192 | bytes 49152 | tf_op jit(solution)/shard_map/add | solution.py:201
  203.8 5.1 all_gather.49
  212.8 9.1 all-gather.1
  222.8 6.8 conditional.4
  226.6 2.5 fusion.148
  235.5 45.8 %all-reduce.9.cloned.1.call-done = f32[2,128,1024]{2,1,0:T(8,128)} async-done(((f32[2,128,1024]{2,1,0:T(8,128)}), f32[2,128,1024]{2,1,0:T(8,128)}) %all-reduce.9.cloned.1.call-update) | async-done | bytes 1048592 | tf_op jit(solution)/shard_map/psum | solution.py:189
  283.0 27.7 %all-gather.23.cloned.1.call-done = bf16[1,1024,1024]{2,1,0:T(8,128)(2,1)} async-done(((bf16[1,128,1024]{2,1,0:T(8,128)(2,1)}), bf16[1,1024,1024]{2,1,0:T(8,128)(2,1)}) %all-gather.23.cloned.1.call-update) | async-done | bytes 2097168 | tf_op jit(solution)/shard_map/all_gather | solution.py:224
  310.6 2.4 fusion.47
  313.0 27.7 %all-gather.25.cloned.1.call-done = bf16[1,1024,1024]{2,1,0:T(8,128)(2,1)} async-done(((bf16[1,128,1024]{2,1,0:T(8,128)(2,1)}), bf16[1,1024,1024]{2,1,0:T(8,128)(2,1)}) %all-gather.25.cloned.1.call-update) | async-done | bytes 2097168 | tf_op jit(solution)/shard_map/all_gather | solution.py:225
  340.8 3.4 fusion.26
  345.0 51.3 %all-reduce.11.cloned.1.call-done = f32[2,128,1024]{2,1,0:T(8,128)} async-done(((f32[2,128,1024]{2,1,0:T(8,128)}), f32[2,128,1024]{2,1,0:T(8,128)}) %all-reduce.11.cloned.1.call-update) | async-done | bytes 1048592 | tf_op jit(solution)/shard_map/psum | solution.py:201
  397.9 25.1 %all-gather.27.cloned.1.call-done = bf16[1,1024,3,256]{3,1,2,0:T(8,128)(2,1)} async-done(((bf16[1,128,3,256]{3,1,2,0:T(8,128)(2,1)}), bf16[1,1024,3,256]{3,1,2,0:T(8,128)(2,1)}) %all-gather.27.cloned.1.call-update) | async-done | bytes 1572880 | tf_op jit(solution)/shard_map/all_gather | solution.py:222
  425.9 9.8 all-gather.5
  436.5 6.2 all-gather.19.cloned.1.call-done
  442.7 7.7 conditional.5
  447.4 2.5 fusion.149
  454.4 49.4 %all-reduce.13.cloned.1.call-done = f32[2,128,1024]{2,1,0:T(8,128)} async-done(((f32[2,128,1024]{2,1,0:T(8,128)}), f32[2,128,1024]{2,1,0:T(8,128)}) %all-reduce.13.cloned.1.call-update) | async-done | bytes 1048592 | tf_op jit(solution)/shard_map/psum | solution.py:189
  505.6 27.1 %all-gather.29.cloned.1.call-done = bf16[1,1024,1024]{2,1,0:T(8,128)(2,1)} async-done(((bf16[1,128,1024]{2,1,0:T(8,128)(2,1)}), bf16[1,1024,1024]{2,1,0:T(8,128)(2,1)}) %all-gather.29.cloned.1.call-update) | async-done | bytes 2097168 | tf_op jit(solution)/shard_map/all_gather | solution.py:224
  532.7 3.3 fusion.53
  536.0 26.9 %all-gather.31.cloned.1.call-done = bf16[1,1024,1024]{2,1,0:T(8,128)(2,1)} async-done(((bf16[1,128,1024]{2,1,0:T(8,128)(2,1)}), bf16[1,1024,1024]{2,1,0:T(8,128)(2,1)}) %all-gather.31.cloned.1.call-update) | async-done | bytes 2097168 | tf_op jit(solution)/shard_map/all_gather | solution.py:225
  563.0 3.9 fusion.158
  571.7 49.8 %all-reduce.15.cloned.1.call-done = f32[2,128,1024]{2,1,0:T(8,128)} async-done(((f32[2,128,1024]{2,1,0:T(8,128)}), f32[2,128,1024]{2,1,0:T(8,128)}) %all-reduce.15.cloned.1.call-update) | async-done | bytes 1048592 | tf_op jit(solution)/shard_map/psum | solution.py:271
  621.5 2.4 multiply_reduce_fusion
  629.7 16.5 %conditional.6 = (f32[2,512,2,256]{1,3,0,2:T(8,128)}, f32[1,256]{1,0:T(1,128)}, bf16[2,128,1,256]{3,1,2,0:T(8,128)(2,1)S(1)}) conditional(s32[]{:T(128)} %convert_element_type.234, (f32[2,512,2,256]{1,3,0,2:T(8,128)}, f32[2,128,4,64]{1,3,2,0:T(8,128)S(1)}) %tuple.89, (pred[2,1,128,512]{3,2,0,1:T(8,128)(4,1)}, ...), branch_computations={%region_23.24_spmd.clone, %region_24.25_spmd.clone} | conditional | flops 341704448 | bytes 28077692 | solution.py:133
  634.7 2.4 exponential_select_fusion.3
  642.4 3.1 pad_maximum_fusion.1
  646.1 3.0 copy.120
  649.2 30.6 %reduce-scatter.17.cloned.1.call-done = f32[2,128,2,256]{3,1,2,0:T(8,128)} async-done(((f32[2,512,2,256]{3,1,2,0:T(8,128)}), f32[2,128,2,256]{3,1,2,0:T(8,128)}) %reduce-scatter.17.cloned.1.call-update) | async-done | bytes 524304 | tf_op jit(solution)/shard_map/reduce_scatter | solution.py:296
  681.6 3.0 fusion.44
  684.6 52.0 %all-reduce.17.cloned.1.call-done = f32[2,128,1024]{2,1,0:T(8,128)} async-done(((f32[2,128,1024]{2,1,0:T(8,128)}), f32[2,128,1024]{2,1,0:T(8,128)}) %all-reduce.17.cloned.1.call-update) | async-done | bytes 1048592 | tf_op jit(solution)/shard_map/psum | solution.py:309
  736.6 2.5 multiply_reduce_fusion.1
  746.0 50.7 %all-reduce.19.cloned.1.call-done = f32[2,128,1024]{2,1,0:T(8,128)} async-done(((f32[2,128,1024]{2,1,0:T(8,128)}), f32[2,128,1024]{2,1,0:T(8,128)}) %all-reduce.19.cloned.1.call-update) | async-done | bytes 1048592 | tf_op jit(solution)/shard_map/psum | solution.py:271
  796.7 2.4 multiply_reduce_fusion.2
  804.7 15.0 conditional.7
  807.1 2.4 copy.123
  809.5 2.3 exponential_select_fusion.2
  816.6 3.1 pad_maximum_fusion
  819.8 2.9 copy.124
  822.8 3.7 fusion.18
  826.5 26.8 %reduce-scatter.19.cloned.1.call-done = f32[2,128,2,256]{3,1,2,0:T(8,128)} async-done(((f32[2,512,2,256]{3,1,2,0:T(8,128)}), f32[2,128,2,256]{3,1,2,0:T(8,128)}) %reduce-scatter.19.cloned.1.call-update) | async-done | bytes 524304 | tf_op jit(solution)/shard_map/reduce_scatter | solution.py:296
  855.1 3.0 fusion.41
  858.5 2.4 fusion.60
  860.9 2.4 fusion.59
  863.4 3.3 bitcast_convert_fusion.2
  866.9 3.2 bitcast_convert_fusion.3
  871.2 3.4 fusion.32
  875.8 3.4 bitcast_convert_fusion.1
  882.2 62.4 %all-reduce.21.cloned.1.call-done = (f32[2,128,1024]{2,1,0:T(8,128)}, f32[2,128,1024]{2,1,0:T(8,128)}) async-done(((f32[2,128,1024]{2,1,0:T(8,128)}, f32[2,128,1024]{2,1,0:T(8,128)}), (f32[2,128,1024]{2,1,0:T(8,128)}, f32[2,128,1024]{2,1,0:T(8,128)})) %all-reduce.21.cloned.1.call-update) | async-done | bytes 2097168 | tf_op jit(solution)/shard_map/psum | solution.py:201
  947.6 2.6 reshape.647
  951.8 2.7 reshape.649
  958.7 22.5 %reduce-scatter.27.cloned.1.call-done = bf16[128,256]{1,0:T(8,128)(2,1)} async-done(((bf16[1024,256]{1,0:T(8,128)(2,1)}), bf16[128,256]{1,0:T(8,128)(2,1)}) %reduce-scatter.27.cloned.1.call-update) | async-done | bytes 65552 | tf_op jit(solution)/shard_map/reduce_scatter | solution.py:342
  981.2 37.8 %reduce-scatter.25.cloned.1.call-done = bf16[128,256]{1,0:T(8,128)(2,1)} async-done(((bf16[1024,256]{1,0:T(8,128)(2,1)}), bf16[128,256]{1,0:T(8,128)(2,1)}) %reduce-scatter.25.cloned.1.call-update) | async-done | bytes 65552 | tf_op jit(solution)/shard_map/reduce_scatter | solution.py:342
  1020.6 42.7 %reduce-scatter.31.cloned.1.call-done = bf16[128,1024]{1,0:T(8,128)(2,1)} async-done(((bf16[1024,1024]{1,0:T(8,128)(2,1)}), bf16[128,1024]{1,0:T(8,128)(2,1)}) %reduce-scatter.31.cloned.1.call-update) | async-done | bytes 262160 | tf_op jit(solution)/shard_map/reduce_scatter | solution.py:345
  1063.3 44.4 %reduce-scatter.29.cloned.1.call-done = bf16[128,1024]{1,0:T(8,128)(2,1)} async-done(((bf16[1024,1024]{1,0:T(8,128)(2,1)}), bf16[128,1024]{1,0:T(8,128)(2,1)}) %reduce-scatter.29.cloned.1.call-update) | async-done | bytes 262160 | tf_op jit(solution)/shard_map/reduce_scatter | solution.py:345
  1109.8 42.4 %reduce-scatter.35.cloned.1.call-done = bf16[128,1024]{1,0:T(8,128)(2,1)} async-done(((bf16[1024,1024]{1,0:T(8,128)(2,1)}), bf16[128,1024]{1,0:T(8,128)(2,1)}) %reduce-scatter.35.cloned.1.call-update) | async-done | bytes 262160 | tf_op jit(solution)/shard_map/reduce_scatter | solution.py:351
  1152.1 44.4 %reduce-scatter.33.cloned.1.call-done = bf16[128,1024]{1,0:T(8,128)(2,1)} async-done(((bf16[1024,1024]{1,0:T(8,128)(2,1)}), bf16[128,1024]{1,0:T(8,128)(2,1)}) %reduce-scatter.33.cloned.1.call-update) | async-done | bytes 262160 | tf_op jit(solution)/shard_map/reduce_scatter | solution.py:351
  1201.1 134.4 %reduce-scatter.37.cloned.1.call-done = f32[32,4]{1,0:T(8,128)} async-done(((f32[1024,4]{1,0:T(8,128)}), f32[32,4]{1,0:T(8,128)}) %reduce-scatter.37.cloned.1.call-update) | async-done | bytes 528
  1337.0 133.0 %reduce-scatter.39.cloned.1.call-done = f32[32,20]{1,0:T(8,128)} async-done(((f32[1024,20]{1,0:T(8,128)}), f32[32,20]{1,0:T(8,128)}) %reduce-scatter.39.cloned.1.call-update) | async-done | bytes 2576
  1471.5 36.1 %reduce-scatter.23.cloned.1.call-done = bf16[128,3,256]{2,0,1:T(8,128)(2,1)} async-done(((bf16[1024,3,256]{2,0,1:T(8,128)(2,1)}), bf16[128,3,256]{2,0,1:T(8,128)(2,1)}) %reduce-scatter.23.cloned.1.call-update) | async-done | bytes 196624 | tf_op jit(solution)/shard_map/reduce_scatter | solution.py:336
  1507.6 41.5 %reduce-scatter.21.cloned.1.call-done = bf16[128,3,256]{2,0,1:T(8,128)(2,1)} async-done(((bf16[1024,3,256]{2,0,1:T(8,128)(2,1)}), bf16[128,3,256]{2,0,1:T(8,128)(2,1)}) %reduce-scatter.21.cloned.1.call-update) | async-done | bytes 196624 | tf_op jit(solution)/shard_map/reduce_scatter | solution.py:336
  (422 shorter events, 113.4 us)
Async XLA Ops:
  7.2 193.7 %all-gather.21.cloned.1.call-start = ((), (), s32[]{:S(2)}) async-start(), calls=%async_computation.30 | async-start | bytes 1769472 | tf_op jit(solution)/shard_map/all_gather | solution.py:222
  9.0 213.7 %all-gather.17.cloned.1.call-start = ((), (), s32[]{:S(2)}) async-start(), calls=%async_computation.12 | async-start | bytes 1310720 | tf_op jit(solution)/shard_map/all_gather | solution.py:184
  84.8 72.7 %copy-start.4 = (bf16[2,128,1024]{2,1,0:T(8,128)(2,1)S(1)}, bf16[2,128,1024]{2,1,0:T(8,128)(2,1)}, u32[]{:S(2)}) copy-start(bf16[2,128,1024]{2,1,0:T(8,128)(2,1)} %param.17) | copy-start | bytes 1572868
  157.7 43.2 %copy-start.63 = (f32[2,128]{1,0:T(2,128)}, f32[2,128]{1,0:T(2,128)S(1)}, u32[]{:S(2)}) copy-start(f32[2,128]{1,0:T(2,128)S(1)} %broadcast_multiply_fusion.15) | copy-start | bytes 3076
  158.0 42.9 %copy-start.89 = (f32[2,128]{1,0:T(2,128)}, f32[2,128]{1,0:T(2,128)S(1)}, u32[]{:S(2)}) copy-start(f32[2,128]{1,0:T(2,128)S(1)} %add_rsqrt_fusion.3) | copy-start | bytes 3076
  176.2 24.6 %copy-start.52 = (f32[1024]{0:T(1024)}, f32[1024]{0:T(1024)S(1)}, u32[]{:S(2)}) copy-start(f32[1024]{0:T(1024)S(1)} %get-tuple-element.615) | copy-start | bytes 12292
  176.2 246.8 %copy-start.54 = (f32[1024]{0:T(1024)}, f32[1024]{0:T(1024)S(1)}, u32[]{:S(2)}) copy-start(f32[1024]{0:T(1024)S(1)} %get-tuple-element.613) | copy-start | bytes 12292
  200.9 109.8 %copy-start.84 = (f32[1024]{0:T(1024)}, f32[1024]{0:T(1024)S(1)}, u32[]{:S(2)}) copy-start(f32[1024]{0:T(1024)S(1)} %get-tuple-element.609) | copy-start | bytes 12292
  200.9 222.1 %copy-start.102 = (f32[1024]{0:T(1024)}, f32[1024]{0:T(1024)S(1)}, u32[]{:S(2)}) copy-start(f32[1024]{0:T(1024)S(1)} %get-tuple-element.607) | copy-start | bytes 12292
  200.9 11.9 copy-start.49
  203.8 77.5 %all-reduce.9.cloned.1.call-start = ((), (), s32[]{:S(2)}) async-start(), calls=%async_computation.13 | async-start | bytes 2097152 | tf_op jit(solution)/shard_map/psum | solution.py:189
  221.9 7.7 copy-start.9
  231.0 79.6 %all-gather.23.cloned.1.call-start = ((), (), s32[]{:S(2)}) async-start(), calls=%async_computation.31 | async-start | bytes 2359296 | tf_op jit(solution)/shard_map/all_gather | solution.py:224
  231.9 108.8 %all-gather.25.cloned.1.call-start = ((), (), s32[]{:S(2)}) async-start(), calls=%async_computation.32 | async-start | bytes 2359296 | tf_op jit(solution)/shard_map/all_gather | solution.py:225
  232.8 163.4 %all-reduce.11.cloned.1.call-start = ((), (), s32[]{:S(2)}) async-start(), calls=%async_computation.14 | async-start | bytes 2097152 | tf_op jit(solution)/shard_map/psum | solution.py:201
  282.7 30.3 %copy-start.56 = (f32[2,128]{1,0:T(2,128)}, f32[2,128]{1,0:T(2,128)S(1)}, u32[]{:S(2)}) copy-start(f32[2,128]{1,0:T(2,128)S(1)} %broadcast_multiply_fusion.14) | copy-start | bytes 3076
  283.0 30.0 %copy-start.65 = (f32[2,128]{1,0:T(2,128)}, f32[2,128]{1,0:T(2,128)S(1)}, u32[]{:S(2)}) copy-start(f32[2,128]{1,0:T(2,128)S(1)} %add_rsqrt_fusion.2) | copy-start | bytes 3076
  313.0 31.1 %copy-start.38 = (f32[2,128,1024]{2,1,0:T(8,128)}, f32[2,128,1024]{2,1,0:T(8,128)S(1)}, u32[]{:S(2)}) copy-start(f32[2,128,1024]{2,1,0:T(8,128)S(1)} %fusion.47) | copy-start | bytes 3145732
  344.2 78.8 %all-gather.27.cloned.1.call-start = ((), (), s32[]{:S(2)}) async-start(), calls=%async_computation.33 | async-start | bytes 1769472 | tf_op jit(solution)/shard_map/all_gather | solution.py:222
  344.9 97.7 %all-gather.19.cloned.1.call-start = ((), (), s32[]{:S(2)}) async-start(), calls=%async_computation.15 | async-start | bytes 1310720 | tf_op jit(solution)/shard_map/all_gather | solution.py:184
  397.7 27.4 %copy-start.80 = (f32[2,128]{1,0:T(2,128)}, f32[2,128]{1,0:T(2,128)S(1)}, u32[]{:S(2)}) copy-start(f32[2,128]{1,0:T(2,128)S(1)} %broadcast_multiply_fusion.13) | copy-start | bytes 3076
  397.9 27.9 %copy-start.91 = (f32[2,128]{1,0:T(2,128)}, f32[2,128]{1,0:T(2,128)S(1)}, u32[]{:S(2)}) copy-start(f32[2,128]{1,0:T(2,128)S(1)} %add_rsqrt_fusion.1) | copy-start | bytes 3076
  425.8 78.1 %all-reduce.13.cloned.1.call-start = ((), (), s32[]{:S(2)}) async-start(), calls=%async_computation.16 | async-start | bytes 2097152 | tf_op jit(solution)/shard_map/psum | solution.py:189
  435.7 14.8 copy-start.11
  442.7 4.8 copy-start.51
  450.4 53.5 %copy-start.88 = (f32[1024]{0:T(1024)S(1)}, f32[1024]{0:T(1024)}, u32[]{:S(2)}) copy-start(f32[1024]{0:T(1024)} %get-tuple-element.606) | copy-start | bytes 12292
  450.5 53.4 %copy-start.31 = (bf16[2,128,4,64]{1,3,2,0:T(8,128)(2,1)}, bf16[2,128,4,64]{1,3,2,0:T(8,128)(2,1)S(1)}, u32[]{:S(2)}) copy-start(bf16[2,128,4,64]{1,3,2,0:T(8,128)(2,1)S(1)} %divide_convert_fusion) | copy-start | bytes 393220
  451.8 80.9 %all-gather.29.cloned.1.call-start = ((), (), s32[]{:S(2)}) async-start(), calls=%async_computation.34 | async-start | bytes 2359296 | tf_op jit(solution)/shard_map/all_gather | solution.py:224
  452.4 110.6 %all-gather.31.cloned.1.call-start = ((), (), s32[]{:S(2)}) async-start(), calls=%async_computation.35 | async-start | bytes 2359296 | tf_op jit(solution)/shard_map/all_gather | solution.py:225
  453.1 168.3 %all-reduce.15.cloned.1.call-start = ((), (), s32[]{:S(2)}) async-start(), calls=%async_computation.17 | async-start | bytes 2097152 | tf_op jit(solution)/shard_map/psum | solution.py:271
  503.9 28.8 %copy-start.86 = (f32[1024]{0:T(1024)S(1)}, f32[1024]{0:T(1024)}, u32[]{:S(2)}) copy-start(f32[1024]{0:T(1024)} %get-tuple-element.605) | copy-start | bytes 12292
  505.3 118.6 %copy-start.59 = (f32[2,128]{1,0:T(2,128)}, f32[2,128]{1,0:T(2,128)S(1)}, u32[]{:S(2)}) copy-start(f32[2,128]{1,0:T(2,128)S(1)} %broadcast_multiply_fusion.12) | copy-start | bytes 3076
  505.6 118.3 %copy-start.68 = (f32[2,128]{1,0:T(2,128)}, f32[2,128]{1,0:T(2,128)S(1)}, u32[]{:S(2)}) copy-start(f32[2,128]{1,0:T(2,128)S(1)} %add_rsqrt_fusion) | copy-start | bytes 3076
  569.4 110.3 %reduce-scatter.17.cloned.1.call-start = ((), (), s32[]{:S(2)}) async-start(), calls=%async_computation.18 | async-start | bytes 2621440 | tf_op jit(solution)/shard_map/reduce_scatter | solution.py:296
  646.1 34.7 %copy-start.43 = (bf16[2,128,1,256]{3,1,2,0:T(8,128)(2,1)}, bf16[2,128,1,256]{3,1,2,0:T(8,128)(2,1)S(1)}, u32[]{:S(2)}) copy-start(bf16[2,128,1,256]{3,1,2,0:T(8,128)(2,1)S(1)} %get-tuple-element.586) | copy-start | bytes 393220
  649.2 87.4 %all-reduce.17.cloned.1.call-start = ((), (), s32[]{:S(2)}) async-start(), calls=%async_computation.19 | async-start | bytes 2097152 | tf_op jit(solution)/shard_map/psum | solution.py:309
  680.9 55.7 %copy-start.55 = (f32[1024]{0:T(1024)S(1)}, f32[1024]{0:T(1024)}, u32[]{:S(2)}) copy-start(f32[1024]{0:T(1024)} %copy-done.54) | copy-start | bytes 12292
  684.5 54.5 %copy-start.81 = (f32[2,128]{1,0:T(2,128)S(1)}, f32[2,128]{1,0:T(2,128)}, u32[]{:S(2)}) copy-start(f32[2,128]{1,0:T(2,128)} %copy-done.80) | copy-start | bytes 3076
  684.5 54.5 %copy-start.92 = (f32[2,128]{1,0:T(2,128)S(1)}, f32[2,128]{1,0:T(2,128)}, u32[]{:S(2)}) copy-start(f32[2,128]{1,0:T(2,128)} %copy-done.91) | copy-start | bytes 3076
  684.6 112.1 %all-reduce.19.cloned.1.call-start = ((), (), s32[]{:S(2)}) async-start(), calls=%async_computation.20 | async-start | bytes 2097152 | tf_op jit(solution)/shard_map/psum | solution.py:271
  743.6 53.1 %copy-start.57 = (f32[2,128]{1,0:T(2,128)S(1)}, f32[2,128]{1,0:T(2,128)}, u32[]{:S(2)}) copy-start(f32[2,128]{1,0:T(2,128)} %copy-done.56) | copy-start | bytes 3076
  743.6 53.1 %copy-start.66 = (f32[2,128]{1,0:T(2,128)S(1)}, f32[2,128]{1,0:T(2,128)}, u32[]{:S(2)}) copy-start(f32[2,128]{1,0:T(2,128)} %copy-done.65) | copy-start | bytes 3076
  745.4 108.0 %reduce-scatter.19.cloned.1.call-start = ((), (), s32[]{:S(2)}) async-start(), calls=%async_computation.21 | async-start | bytes 2621440 | tf_op jit(solution)/shard_map/reduce_scatter | solution.py:296
  819.8 34.7 %copy-start.45 = (bf16[2,128,1,256]{3,1,2,0:T(8,128)(2,1)}, bf16[2,128,1,256]{3,1,2,0:T(8,128)(2,1)S(1)}, u32[]{:S(2)}) copy-start(bf16[2,128,1,256]{3,1,2,0:T(8,128)(2,1)S(1)} %get-tuple-element.587) | copy-start | bytes 393220
  822.7 121.8 %all-reduce.21.cloned.1.call-start = ((), (), s32[]{:S(2)}) async-start(), calls=%async_computation.38 | async-start | bytes 4194304 | tf_op jit(solution)/shard_map/psum | solution.py:201
  858.2 5.2 copy-start.60
  858.2 5.2 copy-start.69
  858.2 5.2 copy-start.87
  858.2 123.0 %reduce-scatter.27.cloned.1.call-start = ((), (), s32[]{:S(2)}) async-start(), calls=%async_computation.25 | async-start | bytes 589824 | tf_op jit(solution)/shard_map/reduce_scatter | solution.py:342
  860.9 158.1 %reduce-scatter.25.cloned.1.call-start = ((), (), s32[]{:S(2)}) async-start(), calls=%async_computation.24 | async-start | bytes 589824 | tf_op jit(solution)/shard_map/reduce_scatter | solution.py:342
  863.3 199.9 %reduce-scatter.31.cloned.1.call-start = ((), (), s32[]{:S(2)}) async-start(), calls=%async_computation.27 | async-start | bytes 2359296 | tf_op jit(solution)/shard_map/reduce_scatter | solution.py:345
  866.8 240.9 %reduce-scatter.29.cloned.1.call-start = ((), (), s32[]{:S(2)}) async-start(), calls=%async_computation.26 | async-start | bytes 2359296 | tf_op jit(solution)/shard_map/reduce_scatter | solution.py:345
  870.1 282.0 %reduce-scatter.35.cloned.1.call-start = ((), (), s32[]{:S(2)}) async-start(), calls=%async_computation.29 | async-start | bytes 2359296 | tf_op jit(solution)/shard_map/reduce_scatter | solution.py:351
  874.6 322.0 %reduce-scatter.33.cloned.1.call-start = ((), (), s32[]{:S(2)}) async-start(), calls=%async_computation.28 | async-start | bytes 2359296 | tf_op jit(solution)/shard_map/reduce_scatter | solution.py:351
  879.3 65.2 %copy-start.5 = (bf16[2,128,1024]{2,1,0:T(8,128)(2,1)S(1)}, bf16[2,128,1024]{2,1,0:T(8,128)(2,1)}, u32[]{:S(2)}) copy-start(bf16[2,128,1024]{2,1,0:T(8,128)(2,1)} %param.17) | copy-start | bytes 1572868
  879.3 65.2 %copy-start.53 = (f32[1024]{0:T(1024)S(1)}, f32[1024]{0:T(1024)}, u32[]{:S(2)}) copy-start(f32[1024]{0:T(1024)} %copy-done.52) | copy-start | bytes 12292
  879.4 65.2 %copy-start.64 = (f32[2,128]{1,0:T(2,128)S(1)}, f32[2,128]{1,0:T(2,128)}, u32[]{:S(2)}) copy-start(f32[2,128]{1,0:T(2,128)} %copy-done.63) | copy-start | bytes 3076
  879.4 65.2 %copy-start.90 = (f32[2,128]{1,0:T(2,128)S(1)}, f32[2,128]{1,0:T(2,128)}, u32[]{:S(2)}) copy-start(f32[2,128]{1,0:T(2,128)} %copy-done.89) | copy-start | bytes 3076
  879.4 456.1 %reduce-scatter.37.cloned.1.call-start = ((), (), s32[]{:S(2)}) async-start(), calls=%async_computation.36 | async-start | bytes 540672
  950.3 519.7 %reduce-scatter.39.cloned.1.call-start = ((), (), s32[]{:S(2)}) async-start(), calls=%async_computation.37 | async-start | bytes 540672
  954.6 553.0 %reduce-scatter.23.cloned.1.call-start = ((), (), s32[]{:S(2)}) async-start(), calls=%async_computation.23 | async-start | bytes 1769472 | tf_op jit(solution)/shard_map/reduce_scatter | solution.py:336
  956.7 592.4 %reduce-scatter.21.cloned.1.call-start = ((), (), s32[]{:S(2)}) async-start(), calls=%async_computation.22 | async-start | bytes 1769472 | tf_op jit(solution)/shard_map/reduce_scatter | solution.py:336
  958.7 240.1 %copy-start.33 = (f32[2,128,1024]{2,1,0:T(8,128)S(1)}, f32[2,128,1024]{2,1,0:T(8,128)}, u32[]{:S(2)}) copy-start(f32[2,128,1024]{2,1,0:T(8,128)} %get-tuple-element.616) | copy-start | bytes 3145732
  958.7 240.1 %copy-start.83 = (f32[1024]{0:T(1024)S(1)}, f32[1024]{0:T(1024)}, u32[]{:S(2)}) copy-start(f32[1024]{0:T(1024)} %get-tuple-element.604) | copy-start | bytes 12292
  (68 other events, 156.5 us)
Sparse Core Ops, SparseCore 0:
  10.5 28.6 all-gather.20
  203.9 14.2 all-gather.16
  231.1 50.0 all-reduce.8
  283.6 27.0 all-gather.22
  312.9 27.7 all-gather.24
  344.3 51.8 all-reduce.10
  398.1 24.8 all-gather.26
  425.9 16.6 all-gather.18
  451.9 51.8 all-reduce.12
  505.6 27.0 all-gather.28
  535.2 27.7 all-gather.30
  569.6 51.8 all-reduce.14
  649.3 30.4 reduce-scatter.16
  684.7 51.8 all-reduce.16
  745.5 51.1 all-reduce.18
  822.9 30.4 reduce-scatter.18
  858.3 86.1 all-reduce.20
  948.0 33.1 reduce-scatter.26
  984.9 34.0 reduce-scatter.24
  1022.1 41.0 reduce-scatter.30
  1066.5 41.1 reduce-scatter.28
  1111.0 41.1 reduce-scatter.34
  1155.4 41.1 reduce-scatter.32
  1199.3 136.1 reduce-scatter.36
  1337.7 132.2 reduce-scatter.38
  1473.1 34.3 reduce-scatter.22
  1510.7 38.3 reduce-scatter.20
where the time goes:
time: 1570 us; the launch traced here: 1560 us
  waiting for transfers between devices  1140 us (73%)
  blocking collectives  166 us (11%)
  other arithmetic  96.3 us (6%)
  matrix products  78.5 us (5%)
  local copies, waits for them, and re-layouts  57.6 us (4%)
  between operations  16.5 us (1%)
    unnamed x29, waiting for transfers between devices  270 us
    psum x2, waiting for transfers between devices, forward_layer(): result = mid + lax.psum(down, 'mp') + vec[5]  114 us
    psum x2, waiting for transfers between devices, per_device(): lax.psum(jnp.einsum('cju,xu->cjx', up_gradient_half_precision, up_weight,...  100 us
    psum x2, waiting for transfers between devices, forward_layer(): mid = state + lax.psum(part, 'mp') + vec[4]  95.2 us
    reduce_scatter x2, waiting for transfers between devices, per_device(): lax.psum_scatter(up_weight_gradient.astype(jnp.bfloat16), ('batch', 'ctx'...  87.1 us
    reduce_scatter x2, waiting for transfers between devices, per_device(): lax.psum_scatter(grad_wd.astype(jnp.bfloat16), ('batch', 'ctx'), scatter_...  86.8 us
    reduce_scatter x2, waiting for transfers between devices, per_device(): lax.psum_scatter(query_weight_gradient.astype(jnp.bfloat16), ('batch', 'c...  77.6 us
    all_gather x1, blocking collectives, per_device(): lax.all_gather(biases, ('batch', 'ctx', 'mp'), axis=2, tiled=True)  74.2 us
  transfers between devices with their start and end apart: 27, of which 25 were waited for; matrix products, arithmetic and copies ran while one was open for 8% of the time, Pallas kernels for 0%

commit v1 on v0

--- a/solution.py
+++ b/solution.py
@@ -3,6 +3,7 @@
 import jax.numpy as jnp
 from jax import lax
 from jax.sharding import PartitionSpec as P
+from jax.lax import all_gather
 
 HEADS = 16
 HEAD = 64
@@ -198,7 +199,12 @@
         act, _ = gelu_parts(up_projected)
         act_bf = act.astype(jnp.bfloat16)
         down = jnp.einsum("slf,of->slo", act_bf, w_d, preferred_element_type=jnp.float32)
-        result = mid + lax.psum(down, "mp") + vec[5]
+
+        def put_shards_over_axis(original):
+            m_next = jnp.sum(all_gather(original, "mp"), 0)
+            return m_next
+
+        result = mid + put_shards_over_axis(down) + vec[5]
         return (
             result,
             (

time: 1570 us -> 1640 us (1.045)
  waiting for transfers between devices: 1140 us -> 1220 us
    all_gather x0 -> x2, waiting for transfers between devices: none -> 159 us  [put_shards_over_axis(): m_next = jnp.sum(all_gather(original, 'mp'), 0)]
    psum x2 -> x0, waiting for transfers between devices: 114 us -> none  [forward_layer(): result = mid + lax.psum(down, 'mp') + vec[5]]
    psum x1 -> x2, waiting for transfers between devices: 52 us -> 83.4 us  [per_device(): lax.psum(jnp.einsum('aewu,vwu->aev', packed_projection_gradient, query_we...]
    unnamed x29 -> x30, waiting for transfers between devices: 270 us -> 271 us
  transfers between devices with their start and end apart: 27 -> 28, of which waited for: 25 -> 26; matrix products, arithmetic and copies ran while one was open for 8% -> 7% of each run, Pallas kernels for 0% -> 0%
where the time goes in v1:
time: 1640 us
  waiting for transfers between devices  1220 us (74%)
  blocking collectives  167 us (10%)
  other arithmetic  98 us (6%)
  matrix products  75.1 us (5%)
  local copies, waits for them, and re-layouts  57.1 us (3%)
  between operations  16.7 us (1%)
    unnamed x30, waiting for transfers between devices  271 us
    all_gather x2, waiting for transfers between devices, put_shards_over_axis(): m_next = jnp.sum(all_gather(original, 'mp'), 0)  159 us
    psum x2, waiting for transfers between devices, per_device(): lax.psum(jnp.einsum('cju,xu->cjx', up_gradient_half_precision, up_weight,...  96.4 us
    psum x2, waiting for transfers between devices, forward_layer(): mid = state + lax.psum(part, 'mp') + vec[4]  95.4 us
    reduce_scatter x2, waiting for transfers between devices, per_device(): lax.psum_scatter(up_weight_gradient.astype(jnp.bfloat16), ('batch', 'ctx'...  87.3 us
    reduce_scatter x2, waiting for transfers between devices, per_device(): lax.psum_scatter(grad_wd.astype(jnp.bfloat16), ('batch', 'ctx'), scatter_...  86.7 us
    psum x2, waiting for transfers between devices, per_device(): lax.psum(jnp.einsum('aewu,vwu->aev', packed_projection_gradient, query_we...  83.4 us
    reduce_scatter x2, waiting for transfers between devices, per_device(): lax.psum_scatter(query_weight_gradient.astype(jnp.bfloat16), ('batch', 'c...  78.3 us
  transfers between devices with their start and end apart: 28, of which 26 were waited for; matrix products, arithmetic and copies ran while one was open for 7% of the time, Pallas kernels for 0%

profile of v1, /device:TPU:0, one launch (start us, length us, event | category | flops | bytes accessed | tf_op | source)
XLA Modules:
  0.0 1636.5 jit_solution(6709615223059466036)
XLA Ops:
  10.7 74.2 %all_gather.63 = bf16[2,10,1024]{1,0,2:T(2,128)(2,1)S(1)} all-gather(bf16[2,10,32]{1,0,2:T(2,128)(2,1)S(1)} %copy.109), channel_id=1, replica_groups=mesh['batch'=2,'ctx'=4,'mp'=4] {'batch','ctx','mp'}, dimensions={2}, use_global_device_ids=true | all-gather | bytes 42240 | tf_op jit(solution)/shard_map/all_gather | solution.py:154
  84.8 2.5 fusion.155
  91.6 68.2 %all_gather.62 = bf16[2,2,1024]{1,0,2:T(2,128)(2,1)S(1)} all-gather(bf16[2,2,32]{1,0,2:T(2,128)(2,1)S(1)} %copy.108), channel_id=1, replica_groups=mesh['batch'=2,'ctx'=4,'mp'=4] {'batch','ctx','mp'}, dimensions={2}, use_global_device_ids=true | all-gather | bytes 8448 | tf_op jit(solution)/shard_map/all_gather | solution.py:153
  160.3 18.1 %fusion.103 = (f32[1024]{0:T(1024)S(1)}, f32[1024]{0:T(1024)S(1)}, f32[1024]{0:T(1024)S(1)}, f32[1024]{0:T(1024)S(1)}) fusion(bf16[2,2,1024]{1,0,2:T(2,128)(2,1)S(1)} %all_gather.62), kind=kLoop, calls=%fused_computation.161 | loop fusion | flops 4096 | bytes 24576 | tf_op jit(solution)/shard_map/mul | solution.py:192
  178.4 24.6 %fusion.101 = (f32[1024]{0:T(1024)S(1)}, f32[1024]{0:T(1024)S(1)}, f32[1024]{0:T(1024)S(1)}, f32[1024]{0:T(1024)}, f32[1024]{0:T(1024)S(1)}, /*index=5*/f32[1024]{0:T(1024)S(1)}, f32[1024]{0:T(1024)S(1)}, f32[1024]{0:T(1024)S(1)}) fusion(bf16[2,10,1024]{1,0,2:T(2,128)(2,1)S(1)} %all_gather.63), kind=kLoop, calls=%fused_computation.157 | loop fusion | flops 8192 | bytes 49152 | tf_op jit(solution)/shard_map/add | solution.py:207
  206.0 5.1 all_gather.61
  213.4 9.6 all-gather.1
  223.9 5.6 conditional.4
  226.4 2.5 fusion.148
  235.5 46.0 %all-reduce.7.cloned.1.call-done = f32[2,128,1024]{2,1,0:T(8,128)} async-done(((f32[2,128,1024]{2,1,0:T(8,128)}), f32[2,128,1024]{2,1,0:T(8,128)}) %all-reduce.7.cloned.1.call-update) | async-done | bytes 1048592 | tf_op jit(solution)/shard_map/psum | solution.py:190
  283.2 27.7 %all-gather.27.cloned.1.call-done = bf16[1,1024,1024]{2,1,0:T(8,128)(2,1)} async-done(((bf16[1,128,1024]{2,1,0:T(8,128)(2,1)}), bf16[1,1024,1024]{2,1,0:T(8,128)(2,1)}) %all-gather.27.cloned.1.call-update) | async-done | bytes 2097168 | tf_op jit(solution)/shard_map/all_gather | solution.py:230
  310.9 2.4 fusion.47
  313.3 27.7 %all-gather.29.cloned.1.call-done = bf16[1,1024,1024]{2,1,0:T(8,128)(2,1)} async-done(((bf16[1,128,1024]{2,1,0:T(8,128)(2,1)}), bf16[1,1024,1024]{2,1,0:T(8,128)(2,1)}) %all-gather.29.cloned.1.call-update) | async-done | bytes 2097168 | tf_op jit(solution)/shard_map/all_gather | solution.py:231
  341.0 3.4 fusion.26
  345.2 80.1 %all-gather.31.cloned.1.call-done = f32[8,128,1024]{2,1,0:T(8,128)} async-done(((f32[2,128,1024]{2,1,0:T(8,128)}), f32[8,128,1024]{2,1,0:T(8,128)}) %all-gather.31.cloned.1.call-update) | async-done | bytes 4194320 | tf_op jit(solution)/shard_map/all_gather | solution.py:204
  425.3 2.7 reduce_sum.420
  428.5 22.8 %all-gather.33.cloned.1.call-done = bf16[1,1024,3,256]{3,1,2,0:T(8,128)(2,1)} async-done(((bf16[1,128,3,256]{3,1,2,0:T(8,128)(2,1)}), bf16[1,1024,3,256]{3,1,2,0:T(8,128)(2,1)}) %all-gather.33.cloned.1.call-update) | async-done | bytes 1572880 | tf_op jit(solution)/shard_map/all_gather | solution.py:228
  454.2 9.8 all-gather.6
  464.8 6.2 all-gather.23.cloned.1.call-done
  471.0 6.5 conditional.5
  474.5 2.5 fusion.149
  481.5 49.4 %all-reduce.9.cloned.1.call-done = f32[2,128,1024]{2,1,0:T(8,128)} async-done(((f32[2,128,1024]{2,1,0:T(8,128)}), f32[2,128,1024]{2,1,0:T(8,128)}) %all-reduce.9.cloned.1.call-update) | async-done | bytes 1048592 | tf_op jit(solution)/shard_map/psum | solution.py:190
  532.7 27.7 %all-gather.35.cloned.1.call-done = bf16[1,1024,1024]{2,1,0:T(8,128)(2,1)} async-done(((bf16[1,128,1024]{2,1,0:T(8,128)(2,1)}), bf16[1,1024,1024]{2,1,0:T(8,128)(2,1)}) %all-gather.35.cloned.1.call-update) | async-done | bytes 2097168 | tf_op jit(solution)/shard_map/all_gather | solution.py:230
  560.3 3.3 fusion.53
  563.7 26.4 %all-gather.37.cloned.1.call-done = bf16[1,1024,1024]{2,1,0:T(8,128)(2,1)} async-done(((bf16[1,128,1024]{2,1,0:T(8,128)(2,1)}), bf16[1,1024,1024]{2,1,0:T(8,128)(2,1)}) %all-gather.37.cloned.1.call-update) | async-done | bytes 2097168 | tf_op jit(solution)/shard_map/all_gather | solution.py:231
  590.0 3.9 fusion.158
  596.6 3.8 fusion.18
  602.8 45.7 %all-reduce.11.cloned.1.call-done = f32[2,128,1024]{2,1,0:T(8,128)} async-done(((f32[2,128,1024]{2,1,0:T(8,128)}), f32[2,128,1024]{2,1,0:T(8,128)}) %all-reduce.11.cloned.1.call-update) | async-done | bytes 1048592 | tf_op jit(solution)/shard_map/psum | solution.py:277
  648.6 2.3 multiply_reduce_fusion
  650.9 79.3 %all-gather.39.cloned.1.call-done = f32[8,128,1024]{2,1,0:T(8,128)} async-done(((f32[2,128,1024]{2,1,0:T(8,128)}), f32[8,128,1024]{2,1,0:T(8,128)}) %all-gather.39.cloned.1.call-update) | async-done | bytes 4194320 | tf_op jit(solution)/shard_map/all_gather | solution.py:204
  730.2 3.7 reduce_sum.425
  733.9 3.7 fusion.140
  742.1 16.3 conditional.6
  744.6 2.3 copy.119
  746.9 2.4 exponential_select_fusion.3
  754.7 3.1 pad_maximum_fusion.1
  758.4 3.0 copy.120
  761.4 29.8 %reduce-scatter.17.cloned.1.call-done = f32[2,128,2,256]{3,1,2,0:T(8,128)} async-done(((f32[2,512,2,256]{3,1,2,0:T(8,128)}), f32[2,128,2,256]{3,1,2,0:T(8,128)}) %reduce-scatter.17.cloned.1.call-update) | async-done | bytes 524304 | tf_op jit(solution)/shard_map/reduce_scatter | solution.py:302
  793.0 3.0 fusion.44
  796.0 52.0 %all-reduce.13.cloned.1.call-done = f32[2,128,1024]{2,1,0:T(8,128)} async-done(((f32[2,128,1024]{2,1,0:T(8,128)}), f32[2,128,1024]{2,1,0:T(8,128)}) %all-reduce.13.cloned.1.call-update) | async-done | bytes 1048592 | tf_op jit(solution)/shard_map/psum | solution.py:315
  848.0 2.5 multiply_reduce_fusion.1
  857.4 50.7 %all-reduce.15.cloned.1.call-done = f32[2,128,1024]{2,1,0:T(8,128)} async-done(((f32[2,128,1024]{2,1,0:T(8,128)}), f32[2,128,1024]{2,1,0:T(8,128)}) %all-reduce.15.cloned.1.call-update) | async-done | bytes 1048592 | tf_op jit(solution)/shard_map/psum | solution.py:277
  908.1 2.5 multiply_reduce_fusion.2
  916.2 15.3 conditional.7
  918.9 2.3 copy.123
  921.2 2.3 exponential_select_fusion.2
  928.3 3.1 pad_maximum_fusion
  931.5 3.0 copy.124
  934.5 30.5 %reduce-scatter.19.cloned.1.call-done = f32[2,128,2,256]{3,1,2,0:T(8,128)} async-done(((f32[2,512,2,256]{3,1,2,0:T(8,128)}), f32[2,128,2,256]{3,1,2,0:T(8,128)}) %reduce-scatter.19.cloned.1.call-update) | async-done | bytes 524304 | tf_op jit(solution)/shard_map/reduce_scatter | solution.py:302
  966.8 3.1 fusion.41
  970.0 2.4 fusion.60
  972.5 2.4 fusion.59
  975.0 3.3 bitcast_convert_fusion.2
  990.6 31.4 %all-reduce.17.cloned.1.call-done = f32[2,128,1024]{2,1,0:T(8,128)} async-done(((f32[2,128,1024]{2,1,0:T(8,128)}), f32[2,128,1024]{2,1,0:T(8,128)}) %all-reduce.17.cloned.1.call-update) | async-done | bytes 1048592 | tf_op jit(solution)/shard_map/psum | solution.py:315
  1032.6 26.5 %reduce-scatter.27.cloned.1.call-done = bf16[128,256]{1,0:T(8,128)(2,1)} async-done(((bf16[1024,256]{1,0:T(8,128)(2,1)}), bf16[128,256]{1,0:T(8,128)(2,1)}) %reduce-scatter.27.cloned.1.call-update) | async-done | bytes 65552 | tf_op jit(solution)/shard_map/reduce_scatter | solution.py:348
  1059.1 37.7 %reduce-scatter.25.cloned.1.call-done = bf16[128,256]{1,0:T(8,128)(2,1)} async-done(((bf16[1024,256]{1,0:T(8,128)(2,1)}), bf16[128,256]{1,0:T(8,128)(2,1)}) %reduce-scatter.25.cloned.1.call-update) | async-done | bytes 65552 | tf_op jit(solution)/shard_map/reduce_scatter | solution.py:348
  1098.3 42.9 %reduce-scatter.31.cloned.1.call-done = bf16[128,1024]{1,0:T(8,128)(2,1)} async-done(((bf16[1024,1024]{1,0:T(8,128)(2,1)}), bf16[128,1024]{1,0:T(8,128)(2,1)}) %reduce-scatter.31.cloned.1.call-update) | async-done | bytes 262160 | tf_op jit(solution)/shard_map/reduce_scatter | solution.py:351
  1141.2 44.4 %reduce-scatter.29.cloned.1.call-done = bf16[128,1024]{1,0:T(8,128)(2,1)} async-done(((bf16[1024,1024]{1,0:T(8,128)(2,1)}), bf16[128,1024]{1,0:T(8,128)(2,1)}) %reduce-scatter.29.cloned.1.call-update) | async-done | bytes 262160 | tf_op jit(solution)/shard_map/reduce_scatter | solution.py:351
  1187.7 42.4 %reduce-scatter.35.cloned.1.call-done = bf16[128,1024]{1,0:T(8,128)(2,1)} async-done(((bf16[1024,1024]{1,0:T(8,128)(2,1)}), bf16[128,1024]{1,0:T(8,128)(2,1)}) %reduce-scatter.35.cloned.1.call-update) | async-done | bytes 262160 | tf_op jit(solution)/shard_map/reduce_scatter | solution.py:357
  1230.0 44.3 %reduce-scatter.33.cloned.1.call-done = bf16[128,1024]{1,0:T(8,128)(2,1)} async-done(((bf16[1024,1024]{1,0:T(8,128)(2,1)}), bf16[128,1024]{1,0:T(8,128)(2,1)}) %reduce-scatter.33.cloned.1.call-update) | async-done | bytes 262160 | tf_op jit(solution)/shard_map/reduce_scatter | solution.py:357
  1277.6 135.4 %reduce-scatter.37.cloned.1.call-done = f32[32,4]{1,0:T(8,128)} async-done(((f32[1024,4]{1,0:T(8,128)}), f32[32,4]{1,0:T(8,128)}) %reduce-scatter.37.cloned.1.call-update) | async-done | bytes 528
  1414.5 133.1 %reduce-scatter.39.cloned.1.call-done = f32[32,20]{1,0:T(8,128)} async-done(((f32[1024,20]{1,0:T(8,128)}), f32[32,20]{1,0:T(8,128)}) %reduce-scatter.39.cloned.1.call-update) | async-done | bytes 2576
  1549.1 36.7 %reduce-scatter.23.cloned.1.call-done = bf16[128,3,256]{2,0,1:T(8,128)(2,1)} async-done(((bf16[1024,3,256]{2,0,1:T(8,128)(2,1)}), bf16[128,3,256]{2,0,1:T(8,128)(2,1)}) %reduce-scatter.23.cloned.1.call-update) | async-done | bytes 196624 | tf_op jit(solution)/shard_map/reduce_scatter | solution.py:342
  1585.8 41.6 %reduce-scatter.21.cloned.1.call-done = bf16[128,3,256]{2,0,1:T(8,128)(2,1)} async-done(((bf16[1024,3,256]{2,0,1:T(8,128)(2,1)}), bf16[128,3,256]{2,0,1:T(8,128)(2,1)}) %reduce-scatter.21.cloned.1.call-update) | async-done | bytes 196624 | tf_op jit(solution)/shard_map/reduce_scatter | solution.py:342
  (419 shorter events, 114.8 us)
Async XLA Ops:
  7.2 195.9 %all-gather.25.cloned.1.call-start = ((), (), s32[]{:S(2)}) async-start(), calls=%async_computation.30 | async-start | bytes 1769472 | tf_op jit(solution)/shard_map/all_gather | solution.py:228
  9.0 214.8 %all-gather.21.cloned.1.call-start = ((), (), s32[]{:S(2)}) async-start(), calls=%async_computation.12 | async-start | bytes 1310720 | tf_op jit(solution)/shard_map/all_gather | solution.py:185
  84.8 74.9 %copy-start.4 = (bf16[2,128,1024]{2,1,0:T(8,128)(2,1)S(1)}, bf16[2,128,1024]{2,1,0:T(8,128)(2,1)}, u32[]{:S(2)}) copy-start(bf16[2,128,1024]{2,1,0:T(8,128)(2,1)} %param.17) | copy-start | bytes 1572868
  159.9 43.1 %copy-start.61 = (f32[2,128]{1,0:T(2,128)}, f32[2,128]{1,0:T(2,128)S(1)}, u32[]{:S(2)}) copy-start(f32[2,128]{1,0:T(2,128)S(1)} %broadcast_multiply_fusion.15) | copy-start | bytes 3076
  160.2 42.9 %copy-start.86 = (f32[2,128]{1,0:T(2,128)}, f32[2,128]{1,0:T(2,128)S(1)}, u32[]{:S(2)}) copy-start(f32[2,128]{1,0:T(2,128)S(1)} %add_rsqrt_fusion.3) | copy-start | bytes 3076
  178.4 24.6 %copy-start.50 = (f32[1024]{0:T(1024)}, f32[1024]{0:T(1024)S(1)}, u32[]{:S(2)}) copy-start(f32[1024]{0:T(1024)S(1)} %get-tuple-element.615) | copy-start | bytes 12292
  178.4 272.9 %copy-start.52 = (f32[1024]{0:T(1024)}, f32[1024]{0:T(1024)S(1)}, u32[]{:S(2)}) copy-start(f32[1024]{0:T(1024)S(1)} %get-tuple-element.613) | copy-start | bytes 12292
  203.0 107.8 %copy-start.79 = (f32[1024]{0:T(1024)}, f32[1024]{0:T(1024)S(1)}, u32[]{:S(2)}) copy-start(f32[1024]{0:T(1024)S(1)} %get-tuple-element.609) | copy-start | bytes 12292
  203.0 357.3 %copy-start.81 = (f32[1024]{0:T(1024)}, f32[1024]{0:T(1024)S(1)}, u32[]{:S(2)}) copy-start(f32[1024]{0:T(1024)S(1)} %get-tuple-element.605) | copy-start | bytes 12292
  203.1 10.3 copy-start.49
  205.9 75.5 %all-reduce.7.cloned.1.call-start = ((), (), s32[]{:S(2)}) async-start(), calls=%async_computation.13 | async-start | bytes 2097152 | tf_op jit(solution)/shard_map/psum | solution.py:190
  211.1 259.9 %copy-start.85 = (s32[128]{0:T(128)}, s32[128]{0:T(128)S(1)}, u32[]{:S(2)}) copy-start(s32[128]{0:T(128)S(1)} %iota_add_fusion) | copy-start | bytes 1540
  213.4 257.6 %copy-start.91 = (f32[4]{0:T(128)}, f32[4]{0:T(128)S(1)}, u32[]{:S(2)}) copy-start(f32[4]{0:T(128)S(1)} %multiply_exponential_fusion) | copy-start | bytes 52
  223.0 6.5 copy-start.9
  230.9 80.0 %all-gather.27.cloned.1.call-start = ((), (), s32[]{:S(2)}) async-start(), calls=%async_computation.31 | async-start | bytes 2359296 | tf_op jit(solution)/shard_map/all_gather | solution.py:230
  231.8 109.2 %all-gather.29.cloned.1.call-start = ((), (), s32[]{:S(2)}) async-start(), calls=%async_computation.32 | async-start | bytes 2359296 | tf_op jit(solution)/shard_map/all_gather | solution.py:231
  232.7 192.6 %all-gather.31.cloned.1.call-start = ((), (), s32[]{:S(2)}) async-start(), calls=%async_computation.33 | async-start | bytes 5242880 | tf_op jit(solution)/shard_map/all_gather | solution.py:204
  282.9 30.3 %copy-start.54 = (f32[2,128]{1,0:T(2,128)}, f32[2,128]{1,0:T(2,128)S(1)}, u32[]{:S(2)}) copy-start(f32[2,128]{1,0:T(2,128)S(1)} %broadcast_multiply_fusion.14) | copy-start | bytes 3076
  283.2 30.1 %copy-start.63 = (f32[2,128]{1,0:T(2,128)}, f32[2,128]{1,0:T(2,128)S(1)}, u32[]{:S(2)}) copy-start(f32[2,128]{1,0:T(2,128)S(1)} %add_rsqrt_fusion.2) | copy-start | bytes 3076
  313.3 31.1 %copy-start.38 = (f32[2,128,1024]{2,1,0:T(8,128)}, f32[2,128,1024]{2,1,0:T(8,128)S(1)}, u32[]{:S(2)}) copy-start(f32[2,128,1024]{2,1,0:T(8,128)S(1)} %fusion.47) | copy-start | bytes 3145732
  344.4 106.9 %all-gather.33.cloned.1.call-start = ((), (), s32[]{:S(2)}) async-start(), calls=%async_computation.34 | async-start | bytes 1769472 | tf_op jit(solution)/shard_map/all_gather | solution.py:228
  345.2 125.8 %all-gather.23.cloned.1.call-start = ((), (), s32[]{:S(2)}) async-start(), calls=%async_computation.14 | async-start | bytes 1310720 | tf_op jit(solution)/shard_map/all_gather | solution.py:185
  428.0 23.3 %copy-start.100 = (f32[1024]{0:T(1024)S(1)}, f32[1024]{0:T(1024)}, u32[]{:S(2)}) copy-start(f32[1024]{0:T(1024)} %get-tuple-element.607) | copy-start | bytes 12292
  428.2 25.1 %copy-start.76 = (f32[2,128]{1,0:T(2,128)}, f32[2,128]{1,0:T(2,128)S(1)}, u32[]{:S(2)}) copy-start(f32[2,128]{1,0:T(2,128)S(1)} %broadcast_multiply_fusion.13) | copy-start | bytes 3076
  428.5 25.6 %copy-start.88 = (f32[2,128]{1,0:T(2,128)}, f32[2,128]{1,0:T(2,128)S(1)}, u32[]{:S(2)}) copy-start(f32[2,128]{1,0:T(2,128)S(1)} %add_rsqrt_fusion.1) | copy-start | bytes 3076
  454.1 76.8 %all-reduce.9.cloned.1.call-start = ((), (), s32[]{:S(2)}) async-start(), calls=%async_computation.15 | async-start | bytes 2097152 | tf_op jit(solution)/shard_map/psum | solution.py:190
  464.0 13.6 copy-start.11
  477.5 53.4 %copy-start.32 = (bf16[2,128,4,64]{1,3,2,0:T(8,128)(2,1)}, bf16[2,128,4,64]{1,3,2,0:T(8,128)(2,1)S(1)}, u32[]{:S(2)}) copy-start(bf16[2,128,4,64]{1,3,2,0:T(8,128)(2,1)S(1)} %divide_convert_fusion) | copy-start | bytes 393220
  478.9 81.4 %all-gather.35.cloned.1.call-start = ((), (), s32[]{:S(2)}) async-start(), calls=%async_computation.35 | async-start | bytes 2359296 | tf_op jit(solution)/shard_map/all_gather | solution.py:230
  479.5 110.6 %all-gather.37.cloned.1.call-start = ((), (), s32[]{:S(2)}) async-start(), calls=%async_computation.36 | async-start | bytes 2359296 | tf_op jit(solution)/shard_map/all_gather | solution.py:231
  480.2 168.3 %all-reduce.11.cloned.1.call-start = ((), (), s32[]{:S(2)}) async-start(), calls=%async_computation.16 | async-start | bytes 2097152 | tf_op jit(solution)/shard_map/psum | solution.py:277
  532.4 201.5 %copy-start.57 = (f32[2,128]{1,0:T(2,128)}, f32[2,128]{1,0:T(2,128)S(1)}, u32[]{:S(2)}) copy-start(f32[2,128]{1,0:T(2,128)S(1)} %broadcast_multiply_fusion.12) | copy-start | bytes 3076
  532.6 201.2 %copy-start.66 = (f32[2,128]{1,0:T(2,128)}, f32[2,128]{1,0:T(2,128)S(1)}, u32[]{:S(2)}) copy-start(f32[2,128]{1,0:T(2,128)S(1)} %add_rsqrt_fusion) | copy-start | bytes 3076
  596.5 133.7 %all-gather.39.cloned.1.call-start = ((), (), s32[]{:S(2)}) async-start(), calls=%async_computation.37 | async-start | bytes 5242880 | tf_op jit(solution)/shard_map/all_gather | solution.py:204
  600.4 190.8 %reduce-scatter.17.cloned.1.call-start = ((), (), s32[]{:S(2)}) async-start(), calls=%async_computation.17 | async-start | bytes 2621440 | tf_op jit(solution)/shard_map/reduce_scatter | solution.py:302
  758.4 33.9 %copy-start.43 = (bf16[2,128,1,256]{3,1,2,0:T(8,128)(2,1)}, bf16[2,128,1,256]{3,1,2,0:T(8,128)(2,1)S(1)}, u32[]{:S(2)}) copy-start(bf16[2,128,1,256]{3,1,2,0:T(8,128)(2,1)S(1)} %get-tuple-element.586) | copy-start | bytes 393220
  761.4 86.7 %all-reduce.13.cloned.1.call-start = ((), (), s32[]{:S(2)}) async-start(), calls=%async_computation.18 | async-start | bytes 2097152 | tf_op jit(solution)/shard_map/psum | solution.py:315
  792.3 55.8 %copy-start.53 = (f32[1024]{0:T(1024)S(1)}, f32[1024]{0:T(1024)}, u32[]{:S(2)}) copy-start(f32[1024]{0:T(1024)} %copy-done.52) | copy-start | bytes 12292
  796.0 54.6 %copy-start.77 = (f32[2,128]{1,0:T(2,128)S(1)}, f32[2,128]{1,0:T(2,128)}, u32[]{:S(2)}) copy-start(f32[2,128]{1,0:T(2,128)} %copy-done.76) | copy-start | bytes 3076
  796.0 54.6 %copy-start.89 = (f32[2,128]{1,0:T(2,128)S(1)}, f32[2,128]{1,0:T(2,128)}, u32[]{:S(2)}) copy-start(f32[2,128]{1,0:T(2,128)} %copy-done.88) | copy-start | bytes 3076
  796.0 112.1 %all-reduce.15.cloned.1.call-start = ((), (), s32[]{:S(2)}) async-start(), calls=%async_computation.19 | async-start | bytes 2097152 | tf_op jit(solution)/shard_map/psum | solution.py:277
  855.1 53.1 %copy-start.55 = (f32[2,128]{1,0:T(2,128)S(1)}, f32[2,128]{1,0:T(2,128)}, u32[]{:S(2)}) copy-start(f32[2,128]{1,0:T(2,128)} %copy-done.54) | copy-start | bytes 3076
  855.1 53.1 %copy-start.64 = (f32[2,128]{1,0:T(2,128)S(1)}, f32[2,128]{1,0:T(2,128)}, u32[]{:S(2)}) copy-start(f32[2,128]{1,0:T(2,128)} %copy-done.63) | copy-start | bytes 3076
  856.8 108.3 %reduce-scatter.19.cloned.1.call-start = ((), (), s32[]{:S(2)}) async-start(), calls=%async_computation.20 | async-start | bytes 2621440 | tf_op jit(solution)/shard_map/reduce_scatter | solution.py:302
  931.5 34.7 %copy-start.45 = (bf16[2,128,1,256]{3,1,2,0:T(8,128)(2,1)}, bf16[2,128,1,256]{3,1,2,0:T(8,128)(2,1)S(1)}, u32[]{:S(2)}) copy-start(bf16[2,128,1,256]{3,1,2,0:T(8,128)(2,1)S(1)} %get-tuple-element.587) | copy-start | bytes 393220
  934.5 87.5 %all-reduce.17.cloned.1.call-start = ((), (), s32[]{:S(2)}) async-start(), calls=%async_computation.21 | async-start | bytes 2097152 | tf_op jit(solution)/shard_map/psum | solution.py:315
  970.0 89.1 %reduce-scatter.27.cloned.1.call-start = ((), (), s32[]{:S(2)}) async-start(), calls=%async_computation.25 | async-start | bytes 589824 | tf_op jit(solution)/shard_map/reduce_scatter | solution.py:348
  972.4 124.3 %reduce-scatter.25.cloned.1.call-start = ((), (), s32[]{:S(2)}) async-start(), calls=%async_computation.24 | async-start | bytes 589824 | tf_op jit(solution)/shard_map/reduce_scatter | solution.py:348
  974.9 166.3 %reduce-scatter.31.cloned.1.call-start = ((), (), s32[]{:S(2)}) async-start(), calls=%async_computation.27 | async-start | bytes 2359296 | tf_op jit(solution)/shard_map/reduce_scatter | solution.py:351
  978.3 207.3 %reduce-scatter.29.cloned.1.call-start = ((), (), s32[]{:S(2)}) async-start(), calls=%async_computation.26 | async-start | bytes 2359296 | tf_op jit(solution)/shard_map/reduce_scatter | solution.py:351
  981.5 248.5 %reduce-scatter.35.cloned.1.call-start = ((), (), s32[]{:S(2)}) async-start(), calls=%async_computation.29 | async-start | bytes 2359296 | tf_op jit(solution)/shard_map/reduce_scatter | solution.py:357
  984.9 289.4 %reduce-scatter.33.cloned.1.call-start = ((), (), s32[]{:S(2)}) async-start(), calls=%async_computation.28 | async-start | bytes 2359296 | tf_op jit(solution)/shard_map/reduce_scatter | solution.py:357
  988.8 33.2 %copy-start.5 = (bf16[2,128,1024]{2,1,0:T(8,128)(2,1)S(1)}, bf16[2,128,1024]{2,1,0:T(8,128)(2,1)}, u32[]{:S(2)}) copy-start(bf16[2,128,1024]{2,1,0:T(8,128)(2,1)} %param.17) | copy-start | bytes 1572868
  988.8 33.2 %copy-start.51 = (f32[1024]{0:T(1024)S(1)}, f32[1024]{0:T(1024)}, u32[]{:S(2)}) copy-start(f32[1024]{0:T(1024)} %copy-done.50) | copy-start | bytes 12292
  988.8 33.2 %copy-start.62 = (f32[2,128]{1,0:T(2,128)S(1)}, f32[2,128]{1,0:T(2,128)}, u32[]{:S(2)}) copy-start(f32[2,128]{1,0:T(2,128)} %copy-done.61) | copy-start | bytes 3076
  988.8 33.2 %copy-start.87 = (f32[2,128]{1,0:T(2,128)S(1)}, f32[2,128]{1,0:T(2,128)}, u32[]{:S(2)}) copy-start(f32[2,128]{1,0:T(2,128)} %copy-done.86) | copy-start | bytes 3076
  988.8 34.9 %copy-start.72 = (f32[1024]{0:T(1024)S(1)}, f32[1024]{0:T(1024)}, u32[]{:S(2)}) copy-start(f32[1024]{0:T(1024)} %get-tuple-element.588) | copy-start | bytes 12292
  988.9 424.2 %reduce-scatter.37.cloned.1.call-start = ((), (), s32[]{:S(2)}) async-start(), calls=%async_computation.38 | async-start | bytes 540672
  990.6 35.2 %copy-start.70 = (f32[1024]{0:T(1024)S(1)}, f32[1024]{0:T(1024)}, u32[]{:S(2)}) copy-start(f32[1024]{0:T(1024)} %get-tuple-element.600) | copy-start | bytes 12292
  1025.9 521.7 %reduce-scatter.39.cloned.1.call-start = ((), (), s32[]{:S(2)}) async-start(), calls=%async_computation.39 | async-start | bytes 540672
  1028.2 557.6 %reduce-scatter.23.cloned.1.call-start = ((), (), s32[]{:S(2)}) async-start(), calls=%async_computation.23 | async-start | bytes 1769472 | tf_op jit(solution)/shard_map/reduce_scatter | solution.py:342
  1030.5 596.9 %reduce-scatter.21.cloned.1.call-start = ((), (), s32[]{:S(2)}) async-start(), calls=%async_computation.22 | async-start | bytes 1769472 | tf_op jit(solution)/shard_map/reduce_scatter | solution.py:342
  1032.6 243.9 %copy-start.1 = (f32[2,128,1024]{2,1,0:T(8,128)S(1)}, f32[2,128,1024]{2,1,0:T(8,128)}, u32[]{:S(2)}) copy-start(f32[2,128,1024]{2,1,0:T(8,128)} %copy-done) | copy-start | bytes 3145732
  1032.6 243.8 %copy-start.13 = (f32[2,128,1024]{2,1,0:T(8,128)S(1)}, f32[2,128,1024]{2,1,0:T(8,128)}, u32[]{:S(2)}) copy-start(f32[2,128,1024]{2,1,0:T(8,128)} %all-reduce.17.cloned.1.call-done) | copy-start | bytes 3145732
  (68 other events, 155.5 us)
Sparse Core Ops, SparseCore 0:
  10.5 28.6 all-gather.24
  206.1 14.9 all-gather.20
  231.0 50.4 all-reduce.6
  283.8 27.0 all-gather.26
  313.2 27.7 all-gather.28
  344.5 80.7 all-gather.30
  427.2 24.0 all-gather.32
  454.2 16.6 all-gather.22
  479.0 51.8 all-reduce.8
  533.3 27.0 all-gather.34
  562.2 27.7 all-gather.36
  596.6 51.8 all-reduce.10
  650.1 79.9 all-gather.38
  761.5 29.6 reduce-scatter.16
  796.1 51.8 all-reduce.12
  856.9 51.1 all-reduce.14
  934.6 30.4 reduce-scatter.18
  970.1 51.9 all-reduce.16
  1025.7 33.3 reduce-scatter.26
  1062.6 34.1 reduce-scatter.24
  1100.0 41.1 reduce-scatter.30
  1144.5 41.0 reduce-scatter.28
  1188.9 41.1 reduce-scatter.34
  1233.2 41.1 reduce-scatter.32
  1277.1 135.8 reduce-scatter.36
  1415.1 132.4 reduce-scatter.38
  1550.8 35.0 reduce-scatter.22
  1589.1 38.3 reduce-scatter.20
